TPU v7x, 512 devices: a whole 4x4x16 slice. The times are simulated.
512 devices in a mesh: gy: 16 (over x_hi, y, core), gx: 32 (over z, x_lo).
Axes of the slice: x: 4 (x_hi: 2, x_lo: 2; x = x_hi * 2 + x_lo), y: 4, z: 16, core: 2. Of those that a mesh axis runs over, the one named last changes fastest.
Arguments:
- embeddings: bfloat16 [128, 4096, 128], P('gy', 'gx'), may hold values from -180 to 180
- affinity: float32 [4, 128, 4096], P(None, 'gy', 'gx'), may hold values from 0 to 1, as said below
- assignment: int32 [128, 4096], P('gy', 'gx'), may hold values from 0 to 1023
Outputs:
- min_distance: float32 [128, 4096], P('gy', 'gx')
- new_centroids: float32 [1024, 128], replicated
Inputs may be any that keep to these rules, and one draw needn't show every extreme that they name: `affinity`: weight 0 exactly for edges that leave the slab; every other edge weighs 0.05 or more.
All inputs are finite; a program needn't handle non-finite values.
Results may differ from a plain program's by a relative error of at most 0.00045.
Values may be sent and summed in bfloat16 or wider, within the bound.
No kernel may reach another device: no remote copies, remote signals or barrier semaphores. Data moves between devices by JAX's collectives and lax.ppermute only.
A program may use at most 64 MiB of HBM per device.

v0:
```python
import math
import jax
import jax.numpy as jnp
from jax import lax
from jax.sharding import PartitionSpec as P

K = 1024
DEGREE = 4
COEFFS = (0.5, 0.45, 0.35, 0.25, 0.15)


def extended(block, sides, width):
    for axis, dim in sides:
        count = lax.axis_size(axis)
        forward = [(i, i + 1) for i in range(count - 1)]
        backward = [(target, source) for source, target in forward]
        low = lax.ppermute(
            lax.slice_in_dim(block, block.shape[dim] - width, None, axis=dim), axis, forward
        )
        high = lax.ppermute(lax.slice_in_dim(block, 0, width, axis=dim), axis, backward)
        block = jnp.concatenate([low, block, high], axis=dim)
    return block


def degree_of(w_ext):
    w_east, w_south, w_diag, w_anti = (w_ext[0], w_ext[1], w_ext[2], w_ext[3])
    result = w_east[1:-1, 1:-1] + w_east[1:-1, :-2]
    result = result + w_south[1:-1, 1:-1] + w_south[:-2, 1:-1]
    result = result + w_diag[1:-1, 1:-1] + w_diag[:-2, :-2]
    return result + w_anti[1:-1, 1:-1] + w_anti[:-2, 2:]


def edge_sum(w_ext, field):
    w_east, w_south, w_diag, w_anti = (w_ext[0], w_ext[1], w_ext[2], w_ext[3])
    result = w_east[1:-1, 1:-1, None] * field[1:-1, 2:]
    result = result + w_east[1:-1, :-2, None] * field[1:-1, :-2]
    result = result + w_south[1:-1, 1:-1, None] * field[2:, 1:-1]
    result = result + w_south[:-2, 1:-1, None] * field[:-2, 1:-1]
    result = result + w_diag[1:-1, 1:-1, None] * field[2:, 2:]
    result = result + w_diag[:-2, :-2, None] * field[:-2, :-2]
    result = result + w_anti[1:-1, 1:-1, None] * field[2:, :-2]
    return result + w_anti[:-2, 2:, None] * field[:-2, 2:]


def whitening(gram, count):
    lower = jnp.linalg.cholesky(gram)
    identity = jnp.eye(gram.shape[0], dtype=gram.dtype)
    inverse = jax.scipy.linalg.solve_triangular(lower, identity, lower=True)
    return math.sqrt(count) * inverse.T


def on_device(embeddings, affinity, assignment):
    rows, cols, chans = embeddings.shape
    reach_all = DEGREE
    w_width = 1
    w_ext = extended(affinity, (("gy", 1), ("gx", 2)), w_width)
    scale = lax.rsqrt(degree_of(w_ext))[..., None]

    def apply_each(field):
        padded = extended(scale * field, (("gy", 0), ("gx", 1)), 1)
        return scale * edge_sum(w_ext, padded)

    previous = embeddings.astype(jnp.float32)
    current = apply_each(previous)
    filtered = COEFFS[0] * previous + COEFFS[1] * current
    for order in range(2, reach_all + 1):
        following = 2.0 * apply_each(current) - previous
        previous, current = (current, following)
        filtered = filtered + COEFFS[order] * following
    pixels = rows * cols
    flat = filtered.reshape(pixels, chans)
    labels = assignment.reshape(pixels)
    total_pixels = pixels * lax.axis_size("gy") * lax.axis_size("gx")
    clusters = K
    block = 128
    highest = lax.Precision.HIGHEST
    gram_local = lax.dot_general(
        flat, flat, (((0,), (0,)), ((), ())), precision=highest, preferred_element_type=jnp.float32
    )
    gram = lax.psum(gram_local, ("gy", "gx"))
    transform = whitening(gram, total_pixels)
    whitened = jnp.dot(flat, transform, precision=highest, preferred_element_type=jnp.float32)

    def one_block(index):
        first = index * block
        onehot = (labels[:, None] == first + jnp.arange(block, dtype=jnp.int32)[None, :]).astype(
            jnp.float32
        )
        partial_sums = lax.dot_general(
            onehot,
            whitened,
            (((0,), (0,)), ((), ())),
            precision=highest,
            preferred_element_type=jnp.float32,
        )
        return (partial_sums, jnp.sum(onehot, axis=0))

    block_sums, block_counts = lax.map(one_block, jnp.arange(clusters // block, dtype=jnp.int32))
    local_sums = block_sums.reshape(clusters, chans)
    local_counts = block_counts.reshape(clusters)
    sums, counts = lax.psum((local_sums, local_counts), ("gy", "gx"))
    centroids = sums / (counts + 1.0)[:, None]
    norms = jnp.sum(whitened * whitened, axis=1)

    def nearest(index, best):
        centre_part = lax.dynamic_slice_in_dim(centroids, index * block, block, 0)
        cross = lax.dot_general(
            whitened,
            centre_part,
            (((1,), (1,)), ((), ())),
            precision=highest,
            preferred_element_type=jnp.float32,
        )
        part_norms = jnp.sum(centre_part * centre_part, axis=1)
        distance = (norms[:, None] - 2.0 * cross + part_norms[None, :]) / chans
        return jnp.minimum(best, jnp.min(distance, axis=1))

    best = lax.fori_loop(0, clusters // block, nearest, jnp.full((pixels,), jnp.inf, jnp.float32))
    return (best.reshape(rows, cols), centroids)


def solution(mesh):
    return jax.shard_map(
        on_device,
        mesh=mesh,
        in_specs=(P("gy", "gx", None), P(None, "gy", "gx"), P("gy", "gx")),
        out_specs=(P("gy", "gx"), P()),
        check_vma=False,
    )
```

profile of v0, /device:TPU:4, one launch (start us, length us, event | category | flops | bytes accessed | tf_op | source)
XLA Modules:
  0.0 1084.3 jit_solution(14910961055857017236)
XLA Ops:
  8.0 2.0 collective-permute-start
  10.1 7.4 collective-permute-start.1
  19.6 3.1 collective-permute-start.2
  22.7 1.3 collective-permute-start.3
  24.2 4.4 collective-permute-done.3
  29.1 1.9 collective-permute-start.4
  31.0 7.3 collective-permute-start.5
  38.3 1.9 collective-permute-done.5
  40.2 1.3 collective-permute-start.6
  41.5 5.4 collective-permute-start.7
  46.9 1.3 collective-permute-done.7
  48.3 1.7 broadcast_multiply_fusion.2
  50.1 1.9 collective-permute-start.8
  52.0 7.3 collective-permute-start.9
  59.3 1.9 collective-permute-done.9
  61.2 1.3 collective-permute-start.10
  62.5 5.4 collective-permute-start.11
  67.9 1.3 collective-permute-done.11
  69.3 1.7 broadcast_multiply_fusion.1
  71.0 1.9 collective-permute-start.12
  73.0 7.3 collective-permute-start.13
  80.2 1.9 collective-permute-done.13
  83.4 5.7 collective-permute-start.15
  89.2 1.3 collective-permute-done.15
  90.6 1.7 broadcast_multiply_fusion
  92.3 1.9 collective-permute-start.16
  94.3 7.3 collective-permute-start.17
  101.5 1.9 collective-permute-done.17
  103.4 1.3 collective-permute-start.18
  104.7 5.7 collective-permute-start.19
  110.5 1.3 collective-permute-done.19
  111.9 1.7 fusion.14
  113.6 1.6 convolution_bitcast_fusion.1
  115.5 453.4 %all-reduce.3.cloned.1.call-done = f32[128,128]{0,1:T(8,128)} async-done(((f32[128,128]{0,1:T(8,128)}), f32[128,128]{0,1:T(8,128)}) %all-reduce.3.cloned.1.call-update) | async-done | bytes 65552 | tf_op jit(solution)/shard_map/psum | solution.py:80
  569.9 11.7 %cholesky.14 = f32[128,128]{1,0:T(8,128)S(1)} custom-call(f32[128,128]{1,0:T(8,128)S(1)} %fusion.63), custom_call_target="Cholesky" | custom-call | tf_op jit(solution)/shard_map/jit(cholesky)/cholesky | solution.py:46
  582.9 9.8 custom-call.7
  594.3 23.2 %while.26 = (s32[]{:T(128)}, f32[8,128,128]{2,1,0:T(8,128)}, f32[8,128]{1,0:T(8,128)S(1)}, s32[8,128]{1,0:T(8,128)S(1)}, s32[8]{0:T(128)S(1)}, /*index=5*/f32[10...) while((s32[]{:T(128)}, f32[8,128,128]{2,1,0:T(8,128)}, f32[8,128]{1,0:T(8,128)S(1)}, ...), condition=%wide.region_5.6_spmd, body=%wide.region_3.5_spmd.sunk | while | flops 201850880 | bytes 601725 | solution.py:98
  595.6 1.4 fusion.88
  598.5 1.4 fusion.88
  601.4 1.4 fusion.88
  604.3 1.4 fusion.88
  607.2 1.4 fusion.88
  610.1 1.4 fusion.88
  613.0 1.4 fusion.88
  615.9 1.4 fusion.88
  617.6 101.1 %psum.23 = f32[1024]{0:T(1024)S(1)} all-reduce(f32[1024]{0:T(1024)S(1)} %bitcast.54), channel_id=1, replica_groups=mesh['gy'=16,'gx'=32] {'gy','gx'}, use_global_device_ids=true, to_apply=%region_7.8 | all-reduce | flops 1024 | bytes 8192 | tf_op jit(solution)/shard_map/psum | solution.py:101
  718.7 350.4 %all-reduce.5.cloned.1.call-done = f32[1024,128]{1,0:T(8,128)} async-done(((f32[1024,128]{1,0:T(8,128)}), f32[1024,128]{1,0:T(8,128)}) %all-reduce.5.cloned.1.call-update) | async-done | bytes 524304 | tf_op jit(solution)/shard_map/psum | solution.py:101
  1070.3 6.3 while.27
  (117 shorter events, 24.3 us)
Async XLA Ops:
  7.2 561.7 %all-reduce.3.cloned.1.call-start = ((), (), s32[]{:S(2)}) async-start(), calls=%async_computation | async-start | bytes 131072 | tf_op jit(solution)/shard_map/psum | solution.py:80
  8.0 20.6 %copy-start.5 = (f32[4,8,128]{2,1,0:T(8,128)S(1)}, f32[4,8,128]{2,1,0:T(8,128)}, u32[]{:S(2)}) copy-start(f32[4,8,128]{2,1,0:T(8,128)} %param.8) | copy-start | bytes 49156
  8.0 9.5 collective-permute-start
  10.1 18.8 %copy-start = (bf16[8,128,128]{2,1,0:T(8,128)(2,1)S(1)}, bf16[8,128,128]{2,1,0:T(8,128)(2,1)}, u32[]{:S(2)}) copy-start(bf16[8,128,128]{2,1,0:T(8,128)(2,1)} %param.7) | copy-start | bytes 786436
  10.1 8.7 collective-permute-start.1
  19.6 4.7 collective-permute-start.2
  22.7 6.0 collective-permute-start.3
  29.1 9.2 collective-permute-start.4
  31.0 9.1 collective-permute-start.5
  40.2 6.8 collective-permute-start.6
  41.5 6.8 collective-permute-start.7
  50.1 9.2 collective-permute-start.8
  52.0 9.1 collective-permute-start.9
  61.2 6.8 collective-permute-start.10
  62.5 6.8 collective-permute-start.11
  71.0 9.2 collective-permute-start.12
  73.0 9.1 collective-permute-start.13
  82.1 7.0 collective-permute-start.14
  83.4 7.0 collective-permute-start.15
  92.3 9.2 collective-permute-start.16
  94.3 9.1 collective-permute-start.17
  103.4 7.0 collective-permute-start.18
  104.7 7.0 collective-permute-start.19
  115.2 953.8 %all-reduce.5.cloned.1.call-start = ((), (), s32[]{:S(2)}) async-start(), calls=%async_computation.1 | async-start | bytes 1048576 | tf_op jit(solution)/shard_map/psum | solution.py:101
  568.8 1.0 copy-start.3
  593.6 0.7 copy-start.2
  1076.6 0.8 copy-start.1
  1076.7 0.8 copy-start.4
Sparse Core Ops, SparseCore 0:
  115.3 453.4 all-reduce.2
  617.7 451.3 all-reduce.4
where the time goes:
time: 1090 us; the launch traced here: 1080 us
  waiting for transfers between devices  823 us (76%)
  blocking collectives  101 us (9%)
  starting transfers between devices  78.3 us (7%)
  other arithmetic  35.1 us (3%)
  matrix products  18.7 us (2%)
  between operations  14.5 us (1%)
    psum x1, waiting for transfers between devices, on_device(): gram = lax.psum(gram_local, ('gy', 'gx'))  453 us
    psum x1, waiting for transfers between devices, on_device(): sums, counts = lax.psum((local_sums, local_counts), ('gy', 'gx'))  350 us
    psum x1, blocking collectives, on_device(): sums, counts = lax.psum((local_sums, local_counts), ('gy', 'gx'))  101 us
    ppermute x10, starting transfers between devices, extended(): lax.ppermute(lax.slice_in_dim(block, 0, width, axis=dim), axis, backward)  42.9 us
    ppermute x10, starting transfers between devices, extended(): lax.ppermute(lax.slice_in_dim(block, block.shape[dim] - width, None, axis...  35.1 us
  transfers between devices with their start and end apart: 22, of which 13 were waited for; matrix products, arithmetic and copies ran while one was open for 0% of the time, Pallas kernels for 0%

commit v1 on v0

--- a/solution.py
+++ b/solution.py
@@ -77,7 +77,7 @@
     gram_local = lax.dot_general(
         flat, flat, (((0,), (0,)), ((), ())), precision=highest, preferred_element_type=jnp.float32
     )
-    gram = lax.psum(gram_local, ("gy", "gx"))
+    gram = lax.psum(lax.psum(gram_local, "gx"), "gy")
     transform = whitening(gram, total_pixels)
     whitened = jnp.dot(flat, transform, precision=highest, preferred_element_type=jnp.float32)
 

time: 1090 us -> 1040 us (0.954)
  waiting for transfers between devices: 823 us -> 770 us
    psum x1 -> x2, waiting for transfers between devices: 453 us -> 397 us  [on_device(): gram = lax.psum(lax.psum(gram_local, 'gx'), 'gy')]
  transfers between devices with their start and end apart: 22 -> 23, of which waited for: 13 -> 14; matrix products, arithmetic and copies ran while one was open for 0% -> 0% of each run, Pallas kernels for 0% -> 0%
where the time goes in v1:
time: 1040 us
  waiting for transfers between devices  770 us (74%)
  blocking collectives  107 us (10%)
  starting transfers between devices  78.3 us (8%)
  other arithmetic  35.1 us (3%)
  matrix products  18.7 us (2%)
  between operations  14.2 us (1%)
    psum x2, waiting for transfers between devices, on_device(): gram = lax.psum(lax.psum(gram_local, 'gx'), 'gy')  397 us
    psum x1, waiting for transfers between devices, on_device(): sums, counts = lax.psum((local_sums, local_counts), ('gy', 'gx'))  355 us
    psum x1, blocking collectives, on_device(): sums, counts = lax.psum((local_sums, local_counts), ('gy', 'gx'))  107 us
    ppermute x10, starting transfers between devices, extended(): lax.ppermute(lax.slice_in_dim(block, 0, width, axis=dim), axis, backward)  42.9 us
    ppermute x10, starting transfers between devices, extended(): lax.ppermute(lax.slice_in_dim(block, block.shape[dim] - width, None, axis...  35.1 us
  transfers between devices with their start and end apart: 23, of which 14 were waited for; matrix products, arithmetic and copies ran while one was open for 0% of the time, Pallas kernels for 0%

profile of v1, /device:TPU:4, one launch (start us, length us, event | category | flops | bytes accessed | tf_op | source)
XLA Modules:
  0.0 1037.6 jit_solution(1300419834270484589)
XLA Ops:
  8.0 2.0 collective-permute-start
  10.1 7.4 collective-permute-start.1
  19.6 3.1 collective-permute-start.2
  22.7 1.3 collective-permute-start.3
  24.2 4.4 collective-permute-done.3
  29.1 1.9 collective-permute-start.4
  31.0 7.3 collective-permute-start.5
  38.3 1.9 collective-permute-done.5
  40.2 1.3 collective-permute-start.6
  41.5 5.4 collective-permute-start.7
  46.9 1.3 collective-permute-done.7
  48.3 1.7 broadcast_multiply_fusion.2
  50.1 1.9 collective-permute-start.8
  52.0 7.3 collective-permute-start.9
  59.3 1.9 collective-permute-done.9
  62.5 5.4 collective-permute-start.11
  67.9 1.3 collective-permute-done.11
  69.3 1.7 broadcast_multiply_fusion.1
  71.0 1.9 collective-permute-start.12
  73.0 7.3 collective-permute-start.13
  80.2 1.9 collective-permute-done.13
  83.4 5.7 collective-permute-start.15
  89.2 1.3 collective-permute-done.15
  90.6 1.7 broadcast_multiply_fusion
  92.3 1.9 collective-permute-start.16
  94.3 7.3 collective-permute-start.17
  101.5 1.9 collective-permute-done.17
  103.4 1.3 collective-permute-start.18
  104.7 5.7 collective-permute-start.19
  110.5 1.3 collective-permute-done.19
  111.9 1.7 fusion.14
  113.6 1.6 convolution_bitcast_fusion.1
  115.3 260.2 %all-reduce.4.cloned.1.call-done = f32[128,128]{0,1:T(8,128)} async-done(((f32[128,128]{0,1:T(8,128)}), f32[128,128]{0,1:T(8,128)}) %all-reduce.4.cloned.1.call-update) | async-done | bytes 65552 | tf_op jit(solution)/shard_map/psum | solution.py:80
  375.8 136.4 %all-reduce.6.cloned.1.call-done = f32[128,128]{0,1:T(8,128)} async-done(((f32[128,128]{0,1:T(8,128)}), f32[128,128]{0,1:T(8,128)}) %all-reduce.6.cloned.1.call-update) | async-done | bytes 65552 | tf_op jit(solution)/shard_map/psum | solution.py:80
  513.1 11.7 %cholesky.14 = f32[128,128]{1,0:T(8,128)S(1)} custom-call(f32[128,128]{1,0:T(8,128)S(1)} %fusion.63), custom_call_target="Cholesky" | custom-call | tf_op jit(solution)/shard_map/jit(cholesky)/cholesky | solution.py:46
  526.2 9.8 custom-call.7
  537.6 23.2 %while.26 = (s32[]{:T(128)}, f32[8,128,128]{2,1,0:T(8,128)}, f32[8,128]{1,0:T(8,128)S(1)}, s32[8,128]{1,0:T(8,128)S(1)}, s32[8]{0:T(128)S(1)}, /*index=5*/f32[10...) while((s32[]{:T(128)}, f32[8,128,128]{2,1,0:T(8,128)}, f32[8,128]{1,0:T(8,128)S(1)}, ...), condition=%wide.region_6.7_spmd, body=%wide.region_4.6_spmd.sunk | while | flops 201850880 | bytes 601725 | solution.py:98
  538.9 1.4 fusion.88
  541.8 1.4 fusion.88
  544.7 1.4 fusion.88
  547.6 1.4 fusion.88
  550.5 1.4 fusion.88
  553.4 1.4 fusion.88
  556.3 1.4 fusion.88
  559.2 1.4 fusion.88
  560.8 107.0 %psum.31 = f32[1024]{0:T(1024)S(1)} all-reduce(f32[1024]{0:T(1024)S(1)} %bitcast.54), channel_id=1, replica_groups=mesh['gy'=16,'gx'=32] {'gy','gx'}, use_global_device_ids=true, to_apply=%region_8.9 | all-reduce | flops 1024 | bytes 8192 | tf_op jit(solution)/shard_map/psum | solution.py:101
  667.8 354.8 %all-reduce.8.cloned.1.call-done = f32[1024,128]{1,0:T(8,128)} async-done(((f32[1024,128]{1,0:T(8,128)}), f32[1024,128]{1,0:T(8,128)}) %all-reduce.8.cloned.1.call-update) | async-done | bytes 524304 | tf_op jit(solution)/shard_map/psum | solution.py:101
  1023.9 6.3 while.27
  (120 shorter events, 25.6 us)
Async XLA Ops:
  7.2 368.3 %all-reduce.4.cloned.1.call-start = ((), (), s32[]{:S(2)}) async-start(), calls=%async_computation | async-start | bytes 131072 | tf_op jit(solution)/shard_map/psum | solution.py:80
  8.0 20.6 %copy-start.5 = (f32[4,8,128]{2,1,0:T(8,128)S(1)}, f32[4,8,128]{2,1,0:T(8,128)}, u32[]{:S(2)}) copy-start(f32[4,8,128]{2,1,0:T(8,128)} %param.8) | copy-start | bytes 49156
  8.0 9.5 collective-permute-start
  10.1 18.8 %copy-start = (bf16[8,128,128]{2,1,0:T(8,128)(2,1)S(1)}, bf16[8,128,128]{2,1,0:T(8,128)(2,1)}, u32[]{:S(2)}) copy-start(bf16[8,128,128]{2,1,0:T(8,128)(2,1)} %param.7) | copy-start | bytes 786436
  10.1 8.7 collective-permute-start.1
  19.6 4.7 collective-permute-start.2
  22.7 6.0 collective-permute-start.3
  29.1 9.2 collective-permute-start.4
  31.0 9.1 collective-permute-start.5
  40.2 6.8 collective-permute-start.6
  41.5 6.8 collective-permute-start.7
  50.1 9.2 collective-permute-start.8
  52.0 9.1 collective-permute-start.9
  61.2 6.8 collective-permute-start.10
  62.5 6.8 collective-permute-start.11
  71.0 9.2 collective-permute-start.12
  73.0 9.1 collective-permute-start.13
  82.1 7.0 collective-permute-start.14
  83.4 7.0 collective-permute-start.15
  92.3 9.2 collective-permute-start.16
  94.3 9.1 collective-permute-start.17
  103.4 7.0 collective-permute-start.18
  104.7 7.0 collective-permute-start.19
  115.2 396.9 %all-reduce.6.cloned.1.call-start = ((), (), s32[]{:S(2)}) async-start(), calls=%async_computation.1 | async-start | bytes 131072 | tf_op jit(solution)/shard_map/psum | solution.py:80
  375.5 647.1 %all-reduce.8.cloned.1.call-start = ((), (), s32[]{:S(2)}) async-start(), calls=%async_computation.2 | async-start | bytes 1048576 | tf_op jit(solution)/shard_map/psum | solution.py:101
  512.1 1.0 copy-start.3
  536.9 0.7 copy-start.2
  1030.2 0.8 copy-start.1
  1030.3 0.8 copy-start.4
Sparse Core Ops, SparseCore 0:
  115.3 260.0 all-reduce.3
  378.7 133.4 all-reduce.5
  560.9 461.6 all-reduce.7
